TPU v7x, 32 devices: a whole 2x2x4 slice. The times are simulated.
32 devices in a mesh: dp: 8 (over y, x, core), rep: 4 (over z).
Axes of the slice: x: 2, y: 2, z: 4, core: 2. Of those that a mesh axis runs over, the one named last changes fastest.
Arguments:
- audio_patches: bfloat16 [2, 64, 228, 256], P(None, ('dp', 'rep')), may hold values from -6 to 6
- clip_lengths: int32 [2, 64], P(None, ('dp', 'rep')), may hold values from 114 to 228, as said below
- video_ids: int32 [2, 64], P(None, ('dp', 'rep')), may hold values from 0 to 31
- image_tokens: bfloat16 [2, 64, 256, 1280], P(None, ('dp', 'rep')), may hold values from -6 to 6
- i_qkv: bfloat16 [1280, 3840], P('dp'), may hold values from -0.15625 to 0.15625
- i_out: bfloat16 [1280, 1280], P('dp'), may hold values from -0.625 to 0.625
- i_up: bfloat16 [1280, 5120], P('dp'), may hold values from -0.15625 to 0.15625
- i_down: bfloat16 [5120, 1280], P('dp'), may hold values from -0.078125 to 0.078125
- i_proj: bfloat16 [1280, 1024], P('dp'), may hold values from -0.15625 to 0.15625
- i_gains: bfloat16 [3, 1280], P(None, 'dp'), may hold values from 0.5 to 1.5
- a_patch: float32 [256, 768], P('dp'), may hold values from -0.375 to 0.375
- a_qkv: float32 [768, 2304], P('dp'), may hold values from -0.21875 to 0.21875
- a_out: float32 [768, 768], P('dp'), may hold values from -0.875 to 0.875
- a_up: float32 [768, 3072], P('dp'), may hold values from -0.21875 to 0.21875
- a_down: float32 [3072, 768], P('dp'), may hold values from -0.109375 to 0.109375
- a_proj: float32 [768, 1024], P('dp'), may hold values from -0.21875 to 0.21875
- a_gains: float32 [3, 768], P(None, 'dp'), may hold values from 0.5 to 1.5
- m_patch: float32 [256, 768], P('dp'), may hold values from -5.722046e-06 to 5.722046e-06
- m_qkv: float32 [768, 2304], P('dp'), may hold values from -5.722046e-06 to 5.722046e-06
- m_out: float32 [768, 768], P('dp'), may hold values from -5.722046e-06 to 5.722046e-06
- m_up: float32 [768, 3072], P('dp'), may hold values from -5.722046e-06 to 5.722046e-06
- m_down: float32 [3072, 768], P('dp'), may hold values from -5.722046e-06 to 5.722046e-06
- m_proj: float32 [768, 1024], P('dp'), may hold values from -5.722046e-06 to 5.722046e-06
- m_gains: float32 [3, 768], P(None, 'dp'), may hold values from -2.2888184e-05 to 2.2888184e-05
- s_patch: float32 [256, 768], P('dp'), may hold values from 1.2405519e-14 to 4.9622077e-14
- s_qkv: float32 [768, 2304], P('dp'), may hold values from 1.2405519e-14 to 4.9622077e-14
- s_out: float32 [768, 768], P('dp'), may hold values from 1.2405519e-14 to 4.9622077e-14
- s_up: float32 [768, 3072], P('dp'), may hold values from 1.2405519e-14 to 4.9622077e-14
- s_down: float32 [3072, 768], P('dp'), may hold values from 1.2405519e-14 to 4.9622077e-14
- s_proj: float32 [768, 1024], P('dp'), may hold values from 1.2405519e-14 to 4.9622077e-14
- s_gains: float32 [3, 768], P(None, 'dp'), may hold values from 1.9848831e-13 to 7.9395323e-13
Outputs:
- loss: float32 [], replicated
- grad_norm: float32 [], replicated
- new_patch: float32 [256, 768], P('dp')
- new_qkv: float32 [768, 2304], P('dp')
- new_out: float32 [768, 768], P('dp')
- new_up: float32 [768, 3072], P('dp')
- new_down: float32 [3072, 768], P('dp')
- new_proj: float32 [768, 1024], P('dp')
- new_gains: float32 [3, 768], P(None, 'dp')
- first_patch: float32 [256, 768], P('dp')
- first_qkv: float32 [768, 2304], P('dp')
- first_out: float32 [768, 768], P('dp')
- first_up: float32 [768, 3072], P('dp')
- first_down: float32 [3072, 768], P('dp')
- first_proj: float32 [768, 1024], P('dp')
- first_gains: float32 [3, 768], P(None, 'dp')
- second_patch: float32 [256, 768], P('dp')
- second_qkv: float32 [768, 2304], P('dp')
- second_out: float32 [768, 768], P('dp')
- second_up: float32 [768, 3072], P('dp')
- second_down: float32 [3072, 768], P('dp')
- second_proj: float32 [768, 1024], P('dp')
- second_gains: float32 [3, 768], P(None, 'dp')
Inputs may be any that keep to these rules, and one draw needn't show every extreme that they name: `clip_lengths`: each clip has 228 or 114 patches; in every micro-batch the first clip has 228 and the second 228 // 2.
All inputs are finite; a program needn't handle non-finite values.
Results may differ from a plain program's by a relative error of at most 0.014.
Values may be sent and summed in bfloat16 or wider, within the bound.
No kernel may reach another device: no remote copies, remote signals or barrier semaphores. Data moves between devices by JAX's collectives and lax.ppermute only.
A program may use at most 256 MiB of HBM per device.

v0:
```python
import jax
import jax.numpy as jnp
from jax import lax
from jax.sharding import PartitionSpec as P

HEADS_A = 12
HEADS_I = 16
LEN = 228
IMG_LEN = 256
MICRO = 2
STEP = 7
HIGHEST = lax.Precision.HIGHEST
NORM_EPS = 1e-06
LOGIT_SCALE = 50.0
CLIP_NORM = 0.01
BETA_ONE = 0.9
BETA_TWO = 0.999
ADAM_EPS = 1e-08
WEIGHT_DECAY = 0.1
RATE_MATRIX = 0.05
RATE_GAIN = 0.3


def to_low(value_in):
    return value_in.astype(jnp.bfloat16)


def normed(resid, gain):
    center = resid - jnp.mean(resid, axis=-1, keepdims=True)
    spread = jnp.mean(center * center, axis=-1, keepdims=True)
    return center * lax.rsqrt(spread + NORM_EPS) * gain


def unit_rows(embed_raw):
    return embed_raw * lax.rsqrt(jnp.sum(embed_raw * embed_raw, axis=-1, keepdims=True) + NORM_EPS)


def matmul(left, right):
    return jnp.einsum("cld,de->cle", left, right, preferred_element_type=jnp.float32)


def matmul_back(left, right):
    return jnp.einsum("cle,de->cld", left, right, preferred_element_type=jnp.float32)


def outer_sum(left, right):
    return jnp.einsum("cld,cle->de", left, right, preferred_element_type=jnp.float32)


def attend(query, keyed, valid, score_scale):
    scores = (
        jnp.einsum("clhd,cmhd->chlm", query, keyed, preferred_element_type=jnp.float32)
        * score_scale
    )
    return jnp.where(valid[:, None, None, :], scores, -1e30)


def layer_forward(resid_in, weights, norm_gains, valid, heads):
    w_qkv, w_out, w_up, w_down = weights
    clip_count, length, feature = resid_in.shape
    head_dim = feature // heads
    h_one = to_low(normed(resid_in, norm_gains[0]))
    qkv = to_low(matmul(h_one, w_qkv)).reshape(clip_count, length, 3, heads, head_dim)
    scores = attend(qkv[:, :, 0], qkv[:, :, 1], valid, head_dim ** (-0.5))
    log_total = jax.nn.logsumexp(scores, axis=-1, keepdims=True)
    attn_probs = jnp.exp(scores - log_total)
    attn_mixed = jnp.einsum(
        "chlm,cmhd->clhd", to_low(attn_probs), qkv[:, :, 2], preferred_element_type=jnp.float32
    )
    attn_mixed = to_low(attn_mixed.reshape(clip_count, length, feature))
    resid_mid = resid_in + matmul(attn_mixed, w_out)
    h_two = to_low(normed(resid_mid, norm_gains[1]))
    pre_act = matmul(h_two, w_up)
    hidden = to_low(jax.nn.gelu(pre_act))
    resid_out = resid_mid + matmul(hidden, w_down)
    return (
        resid_out,
        (h_one, qkv, log_total, attn_mixed, resid_mid, h_two, pre_act, hidden, resid_out),
    )


def pool_embed(resid_out, gain, pool_weight, w_proj):
    pooled = jnp.sum(normed(resid_out, gain) * pool_weight[:, :, None], axis=1)
    embed_raw = jnp.dot(to_low(pooled), w_proj, preferred_element_type=jnp.float32)
    return (unit_rows(embed_raw), pooled, embed_raw)


def contrast(audio, image, ids):
    logits = jnp.dot(audio, image.T, precision=HIGHEST) * LOGIT_SCALE
    count_rows = ids.shape[0]
    same = jnp.arange(count_rows)[:, None] == jnp.arange(count_rows)[None, :]
    allowed = jnp.logical_or(ids[:, None] != ids[None, :], same)
    masked = jnp.where(allowed, logits, -1e30)
    matched = jnp.sum(jnp.where(same, logits, 0.0), axis=1)
    row_lse = jax.nn.logsumexp(masked, axis=1)
    col_lse = jax.nn.logsumexp(masked, axis=0)
    return jnp.sum(row_lse - matched) + jnp.sum(col_lse - matched)


def audio_backward(
    d_embed, patches, resid_in, kept, pooled, embed_raw, weights, norm_gains, valid, pool_weight
):
    w_patch, w_qkv, w_out, w_up, w_down, w_proj = weights
    h_one, qkv, log_total, attn_mixed, resid_mid, h_two, pre_act, hidden, resid_out = kept
    clip_count, length, feature = resid_in.shape
    head_dim = feature // HEADS_A
    score_scale = head_dim ** (-0.5)
    d_raw = to_low(jax.vjp(unit_rows, embed_raw)[1](d_embed)[0])
    g_proj = jnp.dot(to_low(pooled).T, d_raw, preferred_element_type=jnp.float32)
    d_pooled = jnp.dot(d_raw, w_proj.T, preferred_element_type=jnp.float32)
    d_normed = d_pooled[:, None, :] * pool_weight[:, :, None]
    d_out, g_three = jax.vjp(normed, resid_out, norm_gains[2])[1](d_normed)
    d_low = to_low(d_out)
    g_down = outer_sum(hidden, d_low)
    d_hidden = matmul_back(d_low, w_down)
    d_pre = to_low(jax.vjp(jax.nn.gelu, pre_act)[1](d_hidden)[0])
    g_up = outer_sum(h_two, d_pre)
    d_ln_two, g_two = jax.vjp(normed, resid_mid, norm_gains[1])[1](matmul_back(d_pre, w_up))
    d_mid = d_out + d_ln_two
    d_mid_low = to_low(d_mid)
    g_out = outer_sum(attn_mixed, d_mid_low)
    d_mixed = to_low(matmul_back(d_mid_low, w_out)).reshape(clip_count, length, HEADS_A, head_dim)
    query, keyed, values_h = (qkv[:, :, 0], qkv[:, :, 1], qkv[:, :, 2])
    attn_probs = jnp.exp(attend(query, keyed, valid, score_scale) - log_total)
    d_probs = jnp.einsum("clhd,cmhd->chlm", d_mixed, values_h, preferred_element_type=jnp.float32)
    d_values = jnp.einsum(
        "chlm,clhd->cmhd", to_low(attn_probs), d_mixed, preferred_element_type=jnp.float32
    )
    d_scores = to_low(
        attn_probs * (d_probs - jnp.sum(attn_probs * d_probs, axis=-1, keepdims=True))
    )
    d_query = (
        jnp.einsum("chlm,cmhd->clhd", d_scores, keyed, preferred_element_type=jnp.float32)
        * score_scale
    )
    d_keyed = (
        jnp.einsum("chlm,clhd->cmhd", d_scores, query, preferred_element_type=jnp.float32)
        * score_scale
    )
    d_qkv = to_low(
        jnp.stack([d_query, d_keyed, d_values], axis=2).reshape(clip_count, length, 3 * feature)
    )
    g_qkv = outer_sum(h_one, d_qkv)
    d_ln_one, g_one = jax.vjp(normed, resid_in, norm_gains[0])[1](matmul_back(d_qkv, w_qkv))
    d_in = to_low(d_mid + d_ln_one)
    g_patch = outer_sum(patches, d_in)
    return (g_patch, g_qkv, g_out, g_up, g_down, g_proj, jnp.stack([g_one, g_two, g_three]))


def adam_step(weight, gradient, moment_one, moment_two, step_rate, decay):
    first_new = BETA_ONE * moment_one + (1.0 - BETA_ONE) * gradient
    second_new = BETA_TWO * moment_two + (1.0 - BETA_TWO) * gradient * gradient
    fixed_one = first_new / (1.0 - BETA_ONE**STEP)
    fixed_two = second_new / (1.0 - BETA_TWO**STEP)
    update = fixed_one / (jnp.sqrt(fixed_two) + ADAM_EPS) + decay * weight
    return (weight - step_rate * update, first_new, second_new)


def local(
    audio_patches,
    clip_lengths,
    video_ids,
    image_tokens,
    i_qkv,
    i_out,
    i_up,
    i_down,
    i_proj,
    i_gains,
    a_patch,
    a_qkv,
    a_out,
    a_up,
    a_down,
    a_proj,
    a_gains,
    m_patch,
    m_qkv,
    m_out,
    m_up,
    m_down,
    m_proj,
    m_gains,
    s_patch,
    s_qkv,
    s_out,
    s_up,
    s_down,
    s_proj,
    s_gains,
):
    masters = (a_patch, a_qkv, a_out, a_up, a_down, a_proj, a_gains)
    firsts = (m_patch, m_qkv, m_out, m_up, m_down, m_proj, m_gains)
    seconds = (s_patch, s_qkv, s_out, s_up, s_down, s_proj, s_gains)
    all_ids = lax.all_gather(video_ids, ("dp", "rep"), axis=1, tiled=True)
    image_w = (
        lax.all_gather(i_qkv, "dp", axis=0, tiled=True),
        lax.all_gather(i_out, "dp", axis=0, tiled=True),
        lax.all_gather(i_up, "dp", axis=0, tiled=True),
        lax.all_gather(i_down, "dp", axis=0, tiled=True),
        lax.all_gather(i_proj, "dp", axis=0, tiled=True),
        lax.all_gather(i_gains, "dp", axis=1, tiled=True),
    )
    image_g = image_w[5].astype(jnp.float32)
    count_rows = all_ids.shape[1]
    same = jnp.arange(count_rows)[:, None] == jnp.arange(count_rows)[None, :]
    allowed = jnp.logical_or(all_ids[:, :, None] != all_ids[:, None, :], same[None])
    loss_scale = count_rows / jnp.sum(allowed.astype(jnp.float32))
    copies = tuple((to_low(w) for w in masters))
    clip_dev = audio_patches.shape[1]
    start_row = lax.axis_index(("dp", "rep")) * clip_dev
    image_valid = jnp.ones((clip_dev, IMG_LEN), dtype=bool)
    image_pool = jnp.ones((clip_dev, IMG_LEN), jnp.float32) / IMG_LEN
    positions = jnp.arange(LEN)
    loss_sum = 0.0
    accum = None
    for micro in range(MICRO):
        gathered = (
            lax.all_gather(copies[0], "dp", axis=0, tiled=True),
            lax.all_gather(copies[1], "dp", axis=0, tiled=True),
            lax.all_gather(copies[2], "dp", axis=0, tiled=True),
            lax.all_gather(copies[3], "dp", axis=0, tiled=True),
            lax.all_gather(copies[4], "dp", axis=0, tiled=True),
            lax.all_gather(copies[5], "dp", axis=0, tiled=True),
            lax.all_gather(copies[6], "dp", axis=1, tiled=True),
        )
        gains_now = gathered[6].astype(jnp.float32)
        lengths_now = clip_lengths[micro]
        valid = positions[None, :] < lengths_now[:, None]
        pool_weight = valid.astype(jnp.float32) / lengths_now[:, None].astype(jnp.float32)
        patches = audio_patches[micro]
        resid_in = matmul(patches, gathered[0])
        resid_out, kept = layer_forward(resid_in, gathered[1:5], gains_now, valid, HEADS_A)
        audio_embed, pooled, embed_raw = pool_embed(
            resid_out, gains_now[2], pool_weight, gathered[5]
        )
        image_out, unused = layer_forward(
            image_tokens[micro].astype(jnp.float32), image_w[:4], image_g, image_valid, HEADS_I
        )
        image_embed, unused_pool, unused_raw = pool_embed(
            image_out, image_g[2], image_pool, image_w[4]
        )
        audio_all, image_all = (
            lax.all_gather(to_low(audio_embed), ("dp", "rep"), axis=0, tiled=True),
            lax.all_gather(to_low(image_embed), ("dp", "rep"), axis=0, tiled=True),
        )
        image_full = image_all.astype(jnp.float32)
        ids_now = all_ids[micro]

        def micro_loss(audio_in):
            return contrast(audio_in, image_full, ids_now)

        part_loss, contrast_back = jax.vjp(micro_loss, audio_all.astype(jnp.float32))
        loss_sum = loss_sum + part_loss
        d_all = contrast_back(loss_scale)[0]
        d_embed = lax.dynamic_slice_in_dim(d_all, start_row, clip_dev, 0)
        back_weights = (
            lax.all_gather(copies[0], "dp", axis=0, tiled=True),
            lax.all_gather(copies[1], "dp", axis=0, tiled=True),
            lax.all_gather(copies[2], "dp", axis=0, tiled=True),
            lax.all_gather(copies[3], "dp", axis=0, tiled=True),
            lax.all_gather(copies[4], "dp", axis=0, tiled=True),
            lax.all_gather(copies[5], "dp", axis=0, tiled=True),
            lax.all_gather(copies[6], "dp", axis=1, tiled=True),
        )
        grads = audio_backward(
            d_embed,
            patches,
            resid_in,
            kept,
            pooled,
            embed_raw,
            back_weights[:6],
            gains_now,
            valid,
            pool_weight,
        )
        shards = (
            lax.psum_scatter(grads[0], "dp", scatter_dimension=0, tiled=True),
            lax.psum_scatter(grads[1], "dp", scatter_dimension=0, tiled=True),
            lax.psum_scatter(grads[2], "dp", scatter_dimension=0, tiled=True),
            lax.psum_scatter(grads[3], "dp", scatter_dimension=0, tiled=True),
            lax.psum_scatter(grads[4], "dp", scatter_dimension=0, tiled=True),
            lax.psum_scatter(grads[5], "dp", scatter_dimension=0, tiled=True),
            lax.psum_scatter(grads[6], "dp", scatter_dimension=1, tiled=True),
        )
        accum = shards if accum is None else tuple((a + b for a, b in zip(accum, shards)))
    summed = lax.psum(accum, "rep")
    local_squares = sum((jnp.sum(g * g) for g in summed))
    grad_norm = jnp.sqrt(lax.psum(local_squares, "dp"))
    factor = jnp.minimum(1.0, CLIP_NORM / grad_norm)
    results = []
    for index in range(7):
        step_rate = RATE_GAIN if index == 6 else RATE_MATRIX
        decay = 0.0 if index == 6 else WEIGHT_DECAY
        results.append(
            adam_step(
                masters[index],
                summed[index] * factor,
                firsts[index],
                seconds[index],
                step_rate,
                decay,
            )
        )
    new_w = tuple((r[0] for r in results))
    new_one = tuple((r[1] for r in results))
    new_two = tuple((r[2] for r in results))
    loss = loss_sum * loss_scale
    return (
        loss,
        grad_norm,
        new_w[0],
        new_w[1],
        new_w[2],
        new_w[3],
        new_w[4],
        new_w[5],
        new_w[6],
        new_one[0],
        new_one[1],
        new_one[2],
        new_one[3],
        new_one[4],
        new_one[5],
        new_one[6],
        new_two[0],
        new_two[1],
        new_two[2],
        new_two[3],
        new_two[4],
        new_two[5],
        new_two[6],
    )


def solution(mesh):
    placed = (
        P(None, ("dp", "rep"), None, None),
        P(None, ("dp", "rep")),
        P(None, ("dp", "rep")),
        P(None, ("dp", "rep"), None, None),
        P("dp", None),
        P("dp", None),
        P("dp", None),
        P("dp", None),
        P("dp", None),
        P(None, "dp"),
        P("dp", None),
        P("dp", None),
        P("dp", None),
        P("dp", None),
        P("dp", None),
        P("dp", None),
        P(None, "dp"),
        P("dp", None),
        P("dp", None),
        P("dp", None),
        P("dp", None),
        P("dp", None),
        P("dp", None),
        P(None, "dp"),
        P("dp", None),
        P("dp", None),
        P("dp", None),
        P("dp", None),
        P("dp", None),
        P("dp", None),
        P(None, "dp"),
    )
    return jax.shard_map(
        local,
        mesh=mesh,
        in_specs=placed,
        out_specs=(
            P(),
            P(),
            P("dp", None),
            P("dp", None),
            P("dp", None),
            P("dp", None),
            P("dp", None),
            P("dp", None),
            P(None, "dp"),
            P("dp", None),
            P("dp", None),
            P("dp", None),
            P("dp", None),
            P("dp", None),
            P("dp", None),
            P(None, "dp"),
            P("dp", None),
            P("dp", None),
            P("dp", None),
            P("dp", None),
            P("dp", None),
            P("dp", None),
            P(None, "dp"),
        ),
        check_vma=False,
    )
```

profile of v0, /device:TPU:0, one launch (start us, length us, event | category | flops | bytes accessed | tf_op | source)
XLA Modules:
  0.0 1388.9 jit_solution(7028372803511178560)
XLA Ops:
  17.8 12.7 all_gather.72
  31.3 8.8 all-gather.1
  43.6 8.1 all-gather.3
  55.1 68.0 %all-gather = s32[32,2,2]{2,1,0:T(2,128)S(1)} all-gather(s32[1,2,2]{2,1,0:T(2,128)S(1)} %bitcast.448), channel_id=1, replica_groups=mesh['dp'=8,'rep'=4] {'dp','rep'}, dimensions={0}, use_global_device_ids=true | all-gather | bytes 528 | tf_op jit(solution)/shard_map/all_gather | solution.py:195
  125.9 5.5 convolution_convert_fusion
  131.4 4.2 copy.278
  141.4 3.7 convolution_convert_fusion.4
  148.1 3.3 convolution_convert_fusion.1
  151.5 4.6 copy.264
  166.4 7.4 fusion.76
  173.8 7.2 fusion.338
  183.9 3.5 fusion.327
  190.0 67.5 %all-gather.2 = bf16[32,2,1024]{2,1,0:T(2,128)(2,1)S(1)} all-gather(bf16[1,2,1024]{2,1,0:T(2,128)(2,1)S(1)} %fusion.251), channel_id=1, replica_groups=mesh['dp'=8,'rep'=4] {'dp','rep'}, dimensions={0}, use_global_device_ids=true | all-gather | bytes 135168 | tf_op jit(solution)/shard_map/all_gather | solution.py:244
  257.6 11.4 fusion.28
  269.0 6.4 copy.271
  275.3 3.1 multiply_reduce_fusion.1
  280.0 4.1 fusion.129
  284.1 4.8 fusion.332
  291.6 12.1 fusion.31
  303.7 6.5 copy.284
  310.2 3.0 multiply_reduce_fusion
  314.9 3.1 fusion.128
  322.3 37.6 %all-gather.32.cloned.1.call-done = bf16[1280,5120]{1,0:T(8,128)(2,1)} async-done(((bf16[160,5120]{1,0:T(8,128)(2,1)}), bf16[1280,5120]{1,0:T(8,128)(2,1)}) %all-gather.32.cloned.1.call-update) | async-done | bytes 13107216 | tf_op jit(solution)/shard_map/all_gather | solution.py:199
  359.9 76.3 %all-gather.34.cloned.1.call-done = bf16[5120,1280]{1,0:T(8,128)(2,1)} async-done(((bf16[640,1280]{1,0:T(8,128)(2,1)}), bf16[5120,1280]{1,0:T(8,128)(2,1)}) %all-gather.34.cloned.1.call-update) | async-done | bytes 13107216 | tf_op jit(solution)/shard_map/all_gather | solution.py:200
  436.2 26.1 %fusion.333 = (f32[2,256]{1,0:T(2,128)S(1)}, f32[2,256,1280]{2,1,0:T(8,128)}) fusion(f32[2,256,1280]{2,1,0:T(8,128)} %copy-done.26, bf16[5120,1280]{1,0:T(8,128)(2,1)} %all-gather.34.cloned.1.call-done, bf16[1280,5120]{1,0:T(8,128)(2,1)} %all-gather.32.cloned.1.call-done, f32[1280]{0:T(1024)S(1)} %get-tuple-element.142, f32[2,256]{1,0:T(2,128)S(1)} %add_rsqrt_fusion.4, ...), kind=kOutput, calls=%fused_computation.521 | convolution fusion | flops 13449297920 | bytes 31468544 | tf_op jit(solution)/shard_map/cld,de->cle/dot_general | solution.py:39
  464.5 26.0 %fusion.329 = (f32[2,256]{1,0:T(2,128)S(1)}, f32[2,256,1280]{2,1,0:T(8,128)}) fusion(f32[2,256,1280]{2,1,0:T(8,128)} %copy-done.27, bf16[5120,1280]{1,0:T(8,128)(2,1)} %all-gather.34.cloned.1.call-done, bf16[1280,5120]{1,0:T(8,128)(2,1)} %all-gather.32.cloned.1.call-done, f32[2,256]{1,0:T(2,128)S(1)} %add_rsqrt_fusion.1, ...), kind=kOutput, calls=%fused_computation.519 | convolution fusion | flops 13449297920 | bytes 31468544 | tf_op jit(solution)/shard_map/cld,de->cle/dot_general | solution.py:39
  498.2 68.3 %all-gather.4 = bf16[32,2,1024]{2,1,0:T(2,128)(2,1)S(1)} all-gather(bf16[1,2,1024]{2,1,0:T(2,128)(2,1)S(1)} %fusion.252), channel_id=1, replica_groups=mesh['dp'=8,'rep'=4] {'dp','rep'}, dimensions={0}, use_global_device_ids=true | all-gather | bytes 135168 | tf_op jit(solution)/shard_map/all_gather | solution.py:245
  573.1 64.3 %all-gather.6 = bf16[32,2,1024]{2,1,0:T(2,128)(2,1)S(1)} all-gather(bf16[1,2,1024]{2,1,0:T(2,128)(2,1)S(1)} %fusion.254), channel_id=1, replica_groups=mesh['dp'=8,'rep'=4] {'dp','rep'}, dimensions={0}, use_global_device_ids=true | all-gather | bytes 135168 | tf_op jit(solution)/shard_map/all_gather | solution.py:245
  638.0 66.8 %all-gather.5 = bf16[32,2,1024]{2,1,0:T(2,128)(2,1)S(1)} all-gather(bf16[1,2,1024]{2,1,0:T(2,128)(2,1)S(1)} %fusion.253), channel_id=1, replica_groups=mesh['dp'=8,'rep'=4] {'dp','rep'}, dimensions={0}, use_global_device_ids=true | all-gather | bytes 135168 | tf_op jit(solution)/shard_map/all_gather | solution.py:244
  709.8 8.7 fusion.40
  718.6 8.8 fusion.47
  741.6 5.4 multiply_reduce_fusion.2
  758.3 5.4 multiply_reduce_fusion.3
  796.3 4.6 fusion.196
  800.9 5.3 bitcast_add_fusion.2
  806.6 6.6 fusion.193
  813.2 9.9 bitcast_add_fusion
  824.4 4.8 fusion.197
  829.2 5.5 bitcast_add_fusion.1
  835.9 29.7 %reduce-scatter.14.cloned.1.call-done = f32[96,768]{1,0:T(8,128)} async-done(((f32[768,768]{1,0:T(8,128)}), f32[96,768]{1,0:T(8,128)}) %reduce-scatter.14.cloned.1.call-update) | async-done | bytes 294928 | tf_op jit(solution)/shard_map/reduce_scatter | solution.py:281
  865.6 50.0 %reduce-scatter.20.cloned.1.call-done = f32[96,1024]{1,0:T(8,128)} async-done(((f32[768,1024]{1,0:T(8,128)}), f32[96,1024]{1,0:T(8,128)}) %reduce-scatter.20.cloned.1.call-update) | async-done | bytes 393232 | tf_op jit(solution)/shard_map/reduce_scatter | solution.py:284
  915.6 68.9 %reduce-scatter.12.cloned.1.call-done = f32[96,2304]{1,0:T(8,128)} async-done(((f32[768,2304]{1,0:T(8,128)}), f32[96,2304]{1,0:T(8,128)}) %reduce-scatter.12.cloned.1.call-update) | async-done | bytes 884752 | tf_op jit(solution)/shard_map/reduce_scatter | solution.py:280
  984.5 80.3 %reduce-scatter.18.cloned.1.call-done = f32[384,768]{1,0:T(8,128)} async-done(((f32[3072,768]{1,0:T(8,128)}), f32[384,768]{1,0:T(8,128)}) %reduce-scatter.18.cloned.1.call-update) | async-done | bytes 1179664 | tf_op jit(solution)/shard_map/reduce_scatter | solution.py:283
  1064.8 80.3 %reduce-scatter.16.cloned.1.call-done = f32[96,3072]{1,0:T(8,128)} async-done(((f32[768,3072]{1,0:T(8,128)}), f32[96,3072]{1,0:T(8,128)}) %reduce-scatter.16.cloned.1.call-update) | async-done | bytes 1179664 | tf_op jit(solution)/shard_map/reduce_scatter | solution.py:282
  1147.8 34.9 %reduce-scatter.24.cloned.1.call-done = f32[96,3]{1,0:T(8,128)} async-done(((f32[768,3]{1,0:T(8,128)}), f32[96,3]{1,0:T(8,128)}) %reduce-scatter.24.cloned.1.call-update) | async-done | bytes 1168
  1183.6 12.2 psum.62
  1196.3 140.8 %all-reduce.3.cloned.1.call-done = (f32[32,768]{1,0:T(8,128)}, f32[96,2304]{1,0:T(8,128)}, f32[96,768]{1,0:T(8,128)}, f32[96,3072]{1,0:T(8,128)}, f32[384,768]{1,0:T(8,128)}, /*index=5*/f32[96,1024]{1,0:T(8,128)}) async-done(((f32[32,768]{1,0:T(8,128)}, f32[96,2304]{1,0:T(8,128)}, f32[96,768]{1,0:T(8,128)}, f32[96,3072]{1,0:T(8,128)}, f32[384,768]{1,0:T(8,128)}, /*index=5*/f32[96,1024]{1,0:T(8,128)}), ...) | async-done | bytes 4030480 | tf_op jit(solution)/shard_map/psum | solution.py:288
  1350.7 14.2 %psum.63 = f32[]{:T(128)} all-reduce(f32[]{:T(128)S(6)} %add.527), channel_id=1, replica_groups=mesh['dp'=8,'rep'=4] {'dp'}, use_global_device_ids=true, to_apply=%region_105.106 | all-reduce | flops 1 | bytes 8 | tf_op jit(solution)/shard_map/psum | solution.py:290
  (529 shorter events, 160.7 us)
Async XLA Ops:
  7.2 118.6 %all-gather.18.cloned.1.call-start = ((), (), s32[]{:S(2)}) async-start(), calls=%async_computation.7 | async-start | bytes 3981312 | tf_op jit(solution)/shard_map/all_gather | solution.py:220
  9.4 135.7 %all-gather.20.cloned.1.call-start = ((), (), s32[]{:S(2)}) async-start(), calls=%async_computation.8 | async-start | bytes 1327104 | tf_op jit(solution)/shard_map/all_gather | solution.py:221
  11.1 155.2 %all-gather.22.cloned.1.call-start = ((), (), s32[]{:S(2)}) async-start(), calls=%async_computation.9 | async-start | bytes 5308416 | tf_op jit(solution)/shard_map/all_gather | solution.py:222
  12.1 161.7 %all-gather.24.cloned.1.call-start = ((), (), s32[]{:S(2)}) async-start(), calls=%async_computation.10 | async-start | bytes 5308416 | tf_op jit(solution)/shard_map/all_gather | solution.py:223
  13.1 175.0 %all-gather.26.cloned.1.call-start = ((), (), s32[]{:S(2)}) async-start(), calls=%async_computation.11 | async-start | bytes 1769472 | tf_op jit(solution)/shard_map/all_gather | solution.py:224
  13.9 243.7 %all-gather.28.cloned.1.call-start = ((), (), s32[]{:S(2)}) async-start(), calls=%async_computation.12 | async-start | bytes 11059200 | tf_op jit(solution)/shard_map/all_gather | solution.py:197
  14.4 269.7 %all-gather.30.cloned.1.call-start = ((), (), s32[]{:S(2)}) async-start(), calls=%async_computation.13 | async-start | bytes 3686400 | tf_op jit(solution)/shard_map/all_gather | solution.py:198
  15.2 344.7 %all-gather.32.cloned.1.call-start = ((), (), s32[]{:S(2)}) async-start(), calls=%async_computation.14 | async-start | bytes 14745600 | tf_op jit(solution)/shard_map/all_gather | solution.py:199
  16.0 420.2 %all-gather.34.cloned.1.call-start = ((), (), s32[]{:S(2)}) async-start(), calls=%async_computation.15 | async-start | bytes 14745600 | tf_op jit(solution)/shard_map/all_gather | solution.py:200
  16.7 479.1 %all-gather.36.cloned.1.call-start = ((), (), s32[]{:S(2)}) async-start(), calls=%async_computation.16 | async-start | bytes 2949120 | tf_op jit(solution)/shard_map/all_gather | solution.py:201
  17.3 818.6 %reduce-scatter.22.cloned.1.call-start = ((), (), s32[]{:S(2)}) async-start(), calls=%async_computation.22 | async-start | bytes 884736 | tf_op jit(solution)/shard_map/reduce_scatter | solution.py:279
  17.7 34.7 %copy-start.71 = (bf16[1,2,228,256]{3,1,2,0:T(2,128)(2,1)}, bf16[1,2,228,256]{3,1,2,0:T(2,128)(2,1)S(1)}, u32[]{:S(2)}) copy-start(bf16[1,2,228,256]{3,1,2,0:T(2,128)(2,1)S(1)} %get-tuple-element.187) | copy-start | bytes 700420
  17.7 13.6 copy-start.127
  17.7 22.5 %copy-start.132 = (s32[2,2]{1,0:T(2,128)S(1)}, s32[2,2]{1,0:T(2,128)}, u32[]{:S(2)}) copy-start(s32[2,2]{1,0:T(2,128)} %param.32) | copy-start | bytes 52
  31.0 114.1 %copy-start.4 = (f32[2,228,768]{2,1,0:T(8,128)}, f32[2,228,768]{2,1,0:T(8,128)S(1)}, u32[]{:S(2)}) copy-start(f32[2,228,768]{2,1,0:T(8,128)S(1)} %get-tuple-element.230) | copy-start | bytes 4202500
  31.0 94.9 %copy-start.109 = (f32[2,228]{1,0:T(2,128)}, f32[2,228]{1,0:T(2,128)S(1)}, u32[]{:S(2)}) copy-start(f32[2,228]{1,0:T(2,128)S(1)} %broadcast_multiply_fusion.8) | copy-start | bytes 5476
  31.3 94.6 %copy-start.125 = (f32[2,228]{1,0:T(2,128)}, f32[2,228]{1,0:T(2,128)S(1)}, u32[]{:S(2)}) copy-start(f32[2,228]{1,0:T(2,128)S(1)} %fusion.266) | copy-start | bytes 5476
  40.2 107.7 %copy-start.93 = (f32[768]{0:T(1024)}, f32[768]{0:T(1024)S(1)}, u32[]{:S(2)}) copy-start(f32[768]{0:T(1024)S(1)} %get-tuple-element.146) | copy-start | bytes 9220
  40.2 141.0 %copy-start.63 = (f32[768]{0:T(1024)}, f32[768]{0:T(1024)S(1)}, u32[]{:S(2)}) copy-start(f32[768]{0:T(1024)S(1)} %get-tuple-element.145) | copy-start | bytes 9220
  52.9 95.1 %copy-start.106 = (f32[2,228]{1,0:T(2,128)}, f32[2,228]{1,0:T(2,128)S(1)}, u32[]{:S(2)}) copy-start(f32[2,228]{1,0:T(2,128)S(1)} %broadcast_multiply_fusion.11) | copy-start | bytes 5476
  54.3 93.7 %copy-start.115 = (f32[2,228]{1,0:T(2,128)}, f32[2,228]{1,0:T(2,128)S(1)}, u32[]{:S(2)}) copy-start(f32[2,228]{1,0:T(2,128)S(1)} %fusion.263) | copy-start | bytes 5476
  54.9 84.9 %copy-start.104 = (pred[2,228]{1,0:T(4,128)(4,1)}, pred[2,228]{1,0:T(4,128)(4,1)S(1)}, u32[]{:S(2)}) copy-start(pred[2,228]{1,0:T(4,128)(4,1)S(1)} %get-tuple-element.250) | copy-start | bytes 1372
  54.9 105.3 %copy-start.102 = (pred[2,228]{1,0:T(4,128)(4,1)}, pred[2,228]{1,0:T(4,128)(4,1)S(1)}, u32[]{:S(2)}) copy-start(pred[2,228]{1,0:T(4,128)(4,1)S(1)} %get-tuple-element.251) | copy-start | bytes 1372
  147.6 26.2 %copy-start.2 = (f32[2,228,768]{2,1,0:T(8,128)}, f32[2,228,768]{2,1,0:T(8,128)S(1)}, u32[]{:S(2)}) copy-start(f32[2,228,768]{2,1,0:T(8,128)S(1)} %get-tuple-element.234) | copy-start | bytes 4202500
  147.6 18.8 %copy-start.89 = (f32[2,228]{1,0:T(2,128)}, f32[2,228]{1,0:T(2,128)S(1)}, u32[]{:S(2)}) copy-start(f32[2,228]{1,0:T(2,128)S(1)} %broadcast_multiply_fusion.7) | copy-start | bytes 5476
  148.1 18.3 %copy-start.91 = (f32[2,228]{1,0:T(2,128)}, f32[2,228]{1,0:T(2,128)S(1)}, u32[]{:S(2)}) copy-start(f32[2,228]{1,0:T(2,128)S(1)} %fusion.267) | copy-start | bytes 5476
  164.9 16.4 %copy-start.95 = (f32[2,228]{1,0:T(2,128)}, f32[2,228]{1,0:T(2,128)S(1)}, u32[]{:S(2)}) copy-start(f32[2,228]{1,0:T(2,128)S(1)} %broadcast_multiply_fusion.10) | copy-start | bytes 5476
  166.3 15.0 %copy-start.97 = (f32[2,228]{1,0:T(2,128)}, f32[2,228]{1,0:T(2,128)S(1)}, u32[]{:S(2)}) copy-start(f32[2,228]{1,0:T(2,128)S(1)} %fusion.264) | copy-start | bytes 5476
  187.4 383.8 %copy-start.7 = (f32[2,228,768]{2,1,0:T(8,128)}, f32[2,228,768]{2,1,0:T(8,128)S(1)}, u32[]{:S(2)}) copy-start(f32[2,228,768]{2,1,0:T(8,128)S(1)} %get-tuple-element.211) | copy-start | bytes 4202500
  188.1 80.9 %copy-start.111 = (bf16[2,768]{1,0:T(2,128)(2,1)}, bf16[2,768]{1,0:T(2,128)(2,1)S(1)}, u32[]{:S(2)}) copy-start(bf16[2,768]{1,0:T(2,128)(2,1)S(1)} %multiply_reduce_fusion.22) | copy-start | bytes 9220
  495.8 70.8 %copy-start.114 = (s32[64]{0:T(128)S(1)}, s32[64]{0:T(128)}, u32[]{:S(2)}) copy-start(s32[64]{0:T(128)} %get-tuple-element.195) | copy-start | bytes 772
  498.1 73.0 %copy-start.101 = (f32[2,228]{1,0:T(2,128)S(1)}, f32[2,228]{1,0:T(2,128)}, u32[]{:S(2)}) copy-start(f32[2,228]{1,0:T(2,128)} %convert_divide_fusion) | copy-start | bytes 5476
  572.3 65.2 %copy-start.10 = (bf16[768,1024]{1,0:T(8,128)(2,1)S(1)}, bf16[768,1024]{1,0:T(8,128)(2,1)}, u32[]{:S(2)}) copy-start(bf16[768,1024]{1,0:T(8,128)(2,1)} %all-gather.26.cloned.1.call-done) | copy-start | bytes 4718596
  572.5 132.4 %copy-start.113 = (s32[64]{0:T(128)S(1)}, s32[64]{0:T(128)}, u32[]{:S(2)}) copy-start(s32[64]{0:T(128)} %get-tuple-element.194) | copy-start | bytes 772
  704.8 13.7 slice-start.4
  709.8 17.6 %slice-start.6 = ((s8[4718592]{0:T(1024)(128)(4,1)}), s8[4194304]{0:T(1024)(128)(4,1)S(1)}, s32[]{:S(2)}) async-start(s8[4718592]{0:T(1024)(128)(4,1)} %bitcast.411), calls=%async_computation.31 | async-start | bytes 8388608
  787.3 78.3 %reduce-scatter.14.cloned.1.call-start = ((), (), s32[]{:S(2)}) async-start(), calls=%async_computation.18 | async-start | bytes 2654208 | tf_op jit(solution)/shard_map/reduce_scatter | solution.py:281
  791.9 123.7 %reduce-scatter.20.cloned.1.call-start = ((), (), s32[]{:S(2)}) async-start(), calls=%async_computation.21 | async-start | bytes 3538944 | tf_op jit(solution)/shard_map/reduce_scatter | solution.py:284
  796.2 188.3 %reduce-scatter.12.cloned.1.call-start = ((), (), s32[]{:S(2)}) async-start(), calls=%async_computation.17 | async-start | bytes 7962624 | tf_op jit(solution)/shard_map/reduce_scatter | solution.py:280
  806.3 258.6 %reduce-scatter.18.cloned.1.call-start = ((), (), s32[]{:S(2)}) async-start(), calls=%async_computation.20 | async-start | bytes 10616832 | tf_op jit(solution)/shard_map/reduce_scatter | solution.py:283
  823.1 322.0 %reduce-scatter.16.cloned.1.call-start = ((), (), s32[]{:S(2)}) async-start(), calls=%async_computation.19 | async-start | bytes 10616832 | tf_op jit(solution)/shard_map/reduce_scatter | solution.py:282
  834.7 348.0 %reduce-scatter.24.cloned.1.call-start = ((), (), s32[]{:S(2)}) async-start(), calls=%async_computation.23 | async-start | bytes 442368
  835.8 501.3 %all-reduce.3.cloned.1.call-start = ((), (), s32[]{:S(2)}) async-start(), calls=%async_computation.24 | async-start | bytes 8060928 | tf_op jit(solution)/shard_map/psum | solution.py:288
  1145.1 220.5 %copy-start.128 = (f32[3,96]{1,0:T(4,128)S(1)}, f32[3,96]{1,0:T(4,128)}, u32[]{:S(2)}) copy-start(f32[3,96]{1,0:T(4,128)} %param.47) | copy-start | bytes 3460
  1145.1 220.5 %copy-start.130 = (f32[3,96]{1,0:T(4,128)S(1)}, f32[3,96]{1,0:T(4,128)}, u32[]{:S(2)}) copy-start(f32[3,96]{1,0:T(4,128)} %param.54) | copy-start | bytes 3460
  1145.1 220.5 %copy-start.131 = (f32[3,96]{1,0:T(4,128)S(1)}, f32[3,96]{1,0:T(4,128)}, u32[]{:S(2)}) copy-start(f32[3,96]{1,0:T(4,128)} %param.61) | copy-start | bytes 3460
  1145.2 221.1 %copy-start.61 = (f32[96,1024]{1,0:T(8,128)S(1)}, f32[96,1024]{1,0:T(8,128)}, u32[]{:S(2)}) copy-start(f32[96,1024]{1,0:T(8,128)} %param.46) | copy-start | bytes 1179652
  1344.6 24.1 %copy-start.39 = (f32[384,768]{1,0:T(8,128)S(1)}, f32[384,768]{1,0:T(8,128)}, u32[]{:S(2)}) copy-start(f32[384,768]{1,0:T(8,128)} %param.45) | copy-start | bytes 3538948
  (117 other events, 387.4 us)
Sparse Core Ops, SparseCore 0:
  10.5 38.2 all-gather.17
  51.2 24.0 all-gather.19
  77.8 38.9 all-gather.21
  119.1 38.9 all-gather.23
  160.4 25.6 all-gather.25
  187.9 60.9 all-gather.27
  250.8 32.8 all-gather.29
  285.5 74.3 all-gather.31
  361.8 74.3 all-gather.33
  437.9 30.1 all-gather.35
  787.4 32.4 reduce-scatter.21
  823.1 42.4 reduce-scatter.13
  869.4 46.2 reduce-scatter.19
  919.0 65.5 reduce-scatter.11
  988.3 76.4 reduce-scatter.17
  1068.6 76.4 reduce-scatter.15
  1148.9 33.7 reduce-scatter.23
  1185.6 151.4 all-reduce.2
where the time goes:
time: 1400 us; the launch traced here: 1390 us
  waiting for transfers between devices  602 us (43%)
  blocking collectives  391 us (28%)
  matrix products  252 us (18%)
  other arithmetic  62.3 us (4%)
  local copies, waits for them, and re-layouts  53.3 us (4%)
  between operations  27.9 us (2%)
    psum x1, waiting for transfers between devices, local(): summed = lax.psum(accum, 'rep')  141 us
    all_gather x2, blocking collectives, local(): lax.all_gather(to_low(audio_embed), ('dp', 'rep'), axis=0, tiled=True)  134 us
    all_gather x2, blocking collectives, local(): lax.all_gather(to_low(image_embed), ('dp', 'rep'), axis=0, tiled=True)  133 us
    dot_general x16, matrix products, matmul(): jnp.einsum('cld,de->cle', left, right, preferred_element_type=jnp.float32)  116 us
    reduce_scatter x1, waiting for transfers between devices, local(): lax.psum_scatter(grads[3], 'dp', scatter_dimension=0, tiled=True)  80.3 us
    reduce_scatter x1, waiting for transfers between devices, local(): lax.psum_scatter(grads[4], 'dp', scatter_dimension=0, tiled=True)  80.3 us
    all_gather x1, waiting for transfers between devices, local(): lax.all_gather(i_down, 'dp', axis=0, tiled=True)  76.3 us
    reduce_scatter x1, waiting for transfers between devices, local(): lax.psum_scatter(grads[1], 'dp', scatter_dimension=0, tiled=True)  68.9 us
  transfers between devices with their start and end apart: 18, of which 9 were waited for; matrix products, arithmetic and copies ran while one was open for 17% of the time, Pallas kernels for 0%

commit v1 on v0

--- a/solution.py
+++ b/solution.py
@@ -240,9 +240,33 @@
         image_embed, unused_pool, unused_raw = pool_embed(
             image_out, image_g[2], image_pool, image_w[4]
         )
+
+        def choose_space(sheet, lane_axis, row_dim):
+            state_now = lax.axis_size(lane_axis)
+            left_arr, current_value, even = (
+                state_now,
+                lax.axis_index(lane_axis),
+                sheet.shape[row_dim],
+            )
+            tile_out, view_out = (sheet, 1)
+            while view_out < left_arr:
+                tile_out = jnp.concatenate(
+                    [
+                        tile_out,
+                        lax.ppermute(
+                            tile_out,
+                            lane_axis,
+                            list(map(lambda at: (at, (at - view_out) % left_arr), range(left_arr))),
+                        ),
+                    ],
+                    row_dim,
+                )
+                view_out = 2 * view_out
+            return jnp.roll(tile_out, shift=current_value * even, axis=row_dim)
+
         audio_all, image_all = (
             lax.all_gather(to_low(audio_embed), ("dp", "rep"), axis=0, tiled=True),
-            lax.all_gather(to_low(image_embed), ("dp", "rep"), axis=0, tiled=True),
+            choose_space(to_low(image_embed), ("dp", "rep"), 0),
         )
         image_full = image_all.astype(jnp.float32)
         ids_now = all_ids[micro]

time: 1400 us -> 1350 us (0.964)
  blocking collectives: 391 us -> 258 us
  waiting for transfers between devices: 602 us -> 682 us
    all_gather x2 -> x0, blocking collectives: 133 us -> none  [local(): lax.all_gather(to_low(image_embed), ('dp', 'rep'), axis=0, tiled=True)]
    all_gather x1, waiting for transfers between devices: 0.02 us -> 58.2 us  [local(): lax.all_gather(i_qkv, 'dp', axis=0, tiled=True)]
  transfers between devices with their start and end apart: 18 -> 28, of which waited for: 9 -> 16; matrix products, arithmetic and copies ran while one was open for 17% -> 18% of each run, Pallas kernels for 0% -> 0%
where the time goes in v1:
time: 1350 us; the launch traced here: 1340 us
  waiting for transfers between devices  682 us (51%)
  blocking collectives  258 us (19%)
  matrix products  249 us (18%)
  other arithmetic  63.1 us (5%)
  local copies, waits for them, and re-layouts  52.7 us (4%)
  between operations  28.1 us (2%)
    psum x1, waiting for transfers between devices, local(): summed = lax.psum(accum, 'rep')  141 us
    all_gather x2, blocking collectives, local(): lax.all_gather(to_low(audio_embed), ('dp', 'rep'), axis=0, tiled=True)  134 us
    dot_general x16, matrix products, matmul(): jnp.einsum('cld,de->cle', left, right, preferred_element_type=jnp.float32)  116 us
    reduce_scatter x1, waiting for transfers between devices, local(): lax.psum_scatter(grads[3], 'dp', scatter_dimension=0, tiled=True)  80.3 us
    reduce_scatter x1, waiting for transfers between devices, local(): lax.psum_scatter(grads[4], 'dp', scatter_dimension=0, tiled=True)  80.3 us
    all_gather x1, waiting for transfers between devices, local(): lax.all_gather(i_down, 'dp', axis=0, tiled=True)  76.3 us
    reduce_scatter x1, waiting for transfers between devices, local(): lax.psum_scatter(grads[1], 'dp', scatter_dimension=0, tiled=True)  68.9 us
    all_gather x1, blocking collectives, local(): all_ids = lax.all_gather(video_ids, ('dp', 'rep'), axis=1, tiled=True)  68 us
  transfers between devices with their start and end apart: 28, of which 16 were waited for; matrix products, arithmetic and copies ran while one was open for 18% of the time, Pallas kernels for 0%

profile of v1, /device:TPU:0, one launch (start us, length us, event | category | flops | bytes accessed | tf_op | source)
XLA Modules:
  0.0 1343.2 jit_solution(3661724690624586458)
XLA Ops:
  17.8 12.7 all_gather.66
  31.3 8.8 all-gather.1
  43.7 8.0 all-gather.3
  55.1 68.0 %all-gather = s32[32,2,2]{2,1,0:T(2,128)S(1)} all-gather(s32[1,2,2]{2,1,0:T(2,128)S(1)} %bitcast.440), channel_id=1, replica_groups=mesh['dp'=8,'rep'=4] {'dp','rep'}, dimensions={0}, use_global_device_ids=true | all-gather | bytes 528 | tf_op jit(solution)/shard_map/all_gather | solution.py:195
  125.8 5.5 convolution_convert_fusion
  131.4 4.2 copy.278
  140.8 3.7 convolution_convert_fusion.4
  147.5 3.3 convolution_convert_fusion.1
  150.8 4.4 copy.264
  165.7 7.3 fusion.76
  173.0 7.6 fusion.342
  183.2 3.5 fusion.331
  190.2 58.2 %all-gather.26.cloned.1.call-done = bf16[1280,3840]{1,0:T(8,128)(2,1)} async-done(((bf16[160,3840]{1,0:T(8,128)(2,1)}), bf16[1280,3840]{1,0:T(8,128)(2,1)}) %all-gather.26.cloned.1.call-update) | async-done | bytes 9830416 | tf_op jit(solution)/shard_map/all_gather | solution.py:197
  248.4 11.0 fusion.28
  259.4 6.4 copy.271
  265.9 3.0 multiply_reduce_fusion.1
  270.5 4.1 fusion.129
  274.6 8.6 all-gather.28.cloned.1.call-done
  283.2 4.8 fusion.336
  290.7 12.1 fusion.31
  302.7 6.5 copy.284
  313.9 3.1 fusion.128
  321.3 38.1 %all-gather.30.cloned.1.call-done = bf16[1280,5120]{1,0:T(8,128)(2,1)} async-done(((bf16[160,5120]{1,0:T(8,128)(2,1)}), bf16[1280,5120]{1,0:T(8,128)(2,1)}) %all-gather.30.cloned.1.call-update) | async-done | bytes 13107216 | tf_op jit(solution)/shard_map/all_gather | solution.py:199
  359.4 76.3 %all-gather.32.cloned.1.call-done = bf16[5120,1280]{1,0:T(8,128)(2,1)} async-done(((bf16[640,1280]{1,0:T(8,128)(2,1)}), bf16[5120,1280]{1,0:T(8,128)(2,1)}) %all-gather.32.cloned.1.call-update) | async-done | bytes 13107216 | tf_op jit(solution)/shard_map/all_gather | solution.py:200
  435.7 26.1 %fusion.337 = (f32[2,256]{1,0:T(2,128)S(1)}, f32[2,256,1280]{2,1,0:T(8,128)}) fusion(f32[2,256,1280]{2,1,0:T(8,128)} %copy-done.26, bf16[5120,1280]{1,0:T(8,128)(2,1)} %all-gather.32.cloned.1.call-done, bf16[1280,5120]{1,0:T(8,128)(2,1)} %all-gather.30.cloned.1.call-done, f32[1280]{0:T(1024)S(1)} %get-tuple-element.143, f32[2,256]{1,0:T(2,128)S(1)} %add_rsqrt_fusion.4, ...), kind=kOutput, calls=%fused_computation.531 | convolution fusion | flops 13449297920 | bytes 31468544 | tf_op jit(solution)/shard_map/cld,de->cle/dot_general | solution.py:39
  464.0 26.0 %fusion.333 = (f32[2,256]{1,0:T(2,128)S(1)}, f32[2,256,1280]{2,1,0:T(8,128)}) fusion(f32[2,256,1280]{2,1,0:T(8,128)} %copy-done.27, bf16[5120,1280]{1,0:T(8,128)(2,1)} %all-gather.32.cloned.1.call-done, bf16[1280,5120]{1,0:T(8,128)(2,1)} %all-gather.30.cloned.1.call-done, f32[2,256]{1,0:T(2,128)S(1)} %add_rsqrt_fusion.1, ...), kind=kOutput, calls=%fused_computation.529 | convolution fusion | flops 13449297920 | bytes 31468544 | tf_op jit(solution)/shard_map/cld,de->cle/dot_general | solution.py:39
  497.9 3.9 collective-permute-start
  518.4 69.6 %all-gather.2 = bf16[32,2,1024]{2,1,0:T(2,128)(2,1)S(1)} all-gather(bf16[1,2,1024]{2,1,0:T(2,128)(2,1)S(1)} %fusion.253), channel_id=1, replica_groups=mesh['dp'=8,'rep'=4] {'dp','rep'}, dimensions={0}, use_global_device_ids=true | all-gather | bytes 135168 | tf_op jit(solution)/shard_map/all_gather | solution.py:268
  595.4 64.4 %all-gather.4 = bf16[32,2,1024]{2,1,0:T(2,128)(2,1)S(1)} all-gather(bf16[1,2,1024]{2,1,0:T(2,128)(2,1)S(1)} %fusion.254), channel_id=1, replica_groups=mesh['dp'=8,'rep'=4] {'dp','rep'}, dimensions={0}, use_global_device_ids=true | all-gather | bytes 135168 | tf_op jit(solution)/shard_map/all_gather | solution.py:268
  665.5 8.7 fusion.40
  674.3 5.6 fusion.47
  694.2 5.4 multiply_reduce_fusion.2
  711.0 5.4 multiply_reduce_fusion.3
  749.0 4.7 fusion.198
  753.7 5.3 bitcast_add_fusion.2
  759.3 6.6 fusion.193
  765.9 9.9 bitcast_add_fusion
  777.1 4.8 fusion.199
  781.9 5.5 bitcast_add_fusion.1
  788.6 31.4 %reduce-scatter.14.cloned.1.call-done = f32[96,768]{1,0:T(8,128)} async-done(((f32[768,768]{1,0:T(8,128)}), f32[96,768]{1,0:T(8,128)}) %reduce-scatter.14.cloned.1.call-update) | async-done | bytes 294928 | tf_op jit(solution)/shard_map/reduce_scatter | solution.py:305
  820.0 50.0 %reduce-scatter.20.cloned.1.call-done = f32[96,1024]{1,0:T(8,128)} async-done(((f32[768,1024]{1,0:T(8,128)}), f32[96,1024]{1,0:T(8,128)}) %reduce-scatter.20.cloned.1.call-update) | async-done | bytes 393232 | tf_op jit(solution)/shard_map/reduce_scatter | solution.py:308
  870.0 68.9 %reduce-scatter.12.cloned.1.call-done = f32[96,2304]{1,0:T(8,128)} async-done(((f32[768,2304]{1,0:T(8,128)}), f32[96,2304]{1,0:T(8,128)}) %reduce-scatter.12.cloned.1.call-update) | async-done | bytes 884752 | tf_op jit(solution)/shard_map/reduce_scatter | solution.py:304
  938.9 80.3 %reduce-scatter.18.cloned.1.call-done = f32[384,768]{1,0:T(8,128)} async-done(((f32[3072,768]{1,0:T(8,128)}), f32[384,768]{1,0:T(8,128)}) %reduce-scatter.18.cloned.1.call-update) | async-done | bytes 1179664 | tf_op jit(solution)/shard_map/reduce_scatter | solution.py:307
  1019.2 80.3 %reduce-scatter.16.cloned.1.call-done = f32[96,3072]{1,0:T(8,128)} async-done(((f32[768,3072]{1,0:T(8,128)}), f32[96,3072]{1,0:T(8,128)}) %reduce-scatter.16.cloned.1.call-update) | async-done | bytes 1179664 | tf_op jit(solution)/shard_map/reduce_scatter | solution.py:306
  1102.2 34.9 %reduce-scatter.24.cloned.1.call-done = f32[96,3]{1,0:T(8,128)} async-done(((f32[768,3]{1,0:T(8,128)}), f32[96,3]{1,0:T(8,128)}) %reduce-scatter.24.cloned.1.call-update) | async-done | bytes 1168
  1137.9 12.2 psum.62
  1150.7 140.8 %all-reduce.3.cloned.1.call-done = (f32[32,768]{1,0:T(8,128)}, f32[96,2304]{1,0:T(8,128)}, f32[96,768]{1,0:T(8,128)}, f32[96,3072]{1,0:T(8,128)}, f32[384,768]{1,0:T(8,128)}, /*index=5*/f32[96,1024]{1,0:T(8,128)}) async-done(((f32[32,768]{1,0:T(8,128)}, f32[96,2304]{1,0:T(8,128)}, f32[96,768]{1,0:T(8,128)}, f32[96,3072]{1,0:T(8,128)}, f32[384,768]{1,0:T(8,128)}, /*index=5*/f32[96,1024]{1,0:T(8,128)}), ...) | async-done | bytes 4030480 | tf_op jit(solution)/shard_map/psum | solution.py:312
  1305.1 14.2 %psum.63 = f32[]{:T(128)} all-reduce(f32[]{:T(128)S(6)} %add.537), channel_id=1, replica_groups=mesh['dp'=8,'rep'=4] {'dp'}, use_global_device_ids=true, to_apply=%region_105.107 | all-reduce | flops 1 | bytes 8 | tf_op jit(solution)/shard_map/psum | solution.py:314
  (565 shorter events, 181.2 us)
Async XLA Ops:
  7.2 118.6 %all-gather.16.cloned.1.call-start = ((), (), s32[]{:S(2)}) async-start(), calls=%async_computation.7 | async-start | bytes 3981312 | tf_op jit(solution)/shard_map/all_gather | solution.py:220
  9.4 135.0 %all-gather.18.cloned.1.call-start = ((), (), s32[]{:S(2)}) async-start(), calls=%async_computation.8 | async-start | bytes 1327104 | tf_op jit(solution)/shard_map/all_gather | solution.py:221
  11.1 154.5 %all-gather.20.cloned.1.call-start = ((), (), s32[]{:S(2)}) async-start(), calls=%async_computation.9 | async-start | bytes 5308416 | tf_op jit(solution)/shard_map/all_gather | solution.py:222
  12.1 160.9 %all-gather.22.cloned.1.call-start = ((), (), s32[]{:S(2)}) async-start(), calls=%async_computation.10 | async-start | bytes 5308416 | tf_op jit(solution)/shard_map/all_gather | solution.py:223
  13.1 174.4 %all-gather.24.cloned.1.call-start = ((), (), s32[]{:S(2)}) async-start(), calls=%async_computation.11 | async-start | bytes 1769472 | tf_op jit(solution)/shard_map/all_gather | solution.py:224
  13.9 234.5 %all-gather.26.cloned.1.call-start = ((), (), s32[]{:S(2)}) async-start(), calls=%async_computation.12 | async-start | bytes 11059200 | tf_op jit(solution)/shard_map/all_gather | solution.py:197
  14.4 268.7 %all-gather.28.cloned.1.call-start = ((), (), s32[]{:S(2)}) async-start(), calls=%async_computation.13 | async-start | bytes 3686400 | tf_op jit(solution)/shard_map/all_gather | solution.py:198
  15.2 344.2 %all-gather.30.cloned.1.call-start = ((), (), s32[]{:S(2)}) async-start(), calls=%async_computation.14 | async-start | bytes 14745600 | tf_op jit(solution)/shard_map/all_gather | solution.py:199
  16.0 419.8 %all-gather.32.cloned.1.call-start = ((), (), s32[]{:S(2)}) async-start(), calls=%async_computation.15 | async-start | bytes 14745600 | tf_op jit(solution)/shard_map/all_gather | solution.py:200
  16.7 478.6 %all-gather.34.cloned.1.call-start = ((), (), s32[]{:S(2)}) async-start(), calls=%async_computation.16 | async-start | bytes 2949120 | tf_op jit(solution)/shard_map/all_gather | solution.py:201
  17.3 771.3 %reduce-scatter.22.cloned.1.call-start = ((), (), s32[]{:S(2)}) async-start(), calls=%async_computation.22 | async-start | bytes 884736 | tf_op jit(solution)/shard_map/reduce_scatter | solution.py:303
  17.7 34.7 %copy-start.71 = (bf16[1,2,228,256]{3,1,2,0:T(2,128)(2,1)}, bf16[1,2,228,256]{3,1,2,0:T(2,128)(2,1)S(1)}, u32[]{:S(2)}) copy-start(bf16[1,2,228,256]{3,1,2,0:T(2,128)(2,1)S(1)} %get-tuple-element.188) | copy-start | bytes 700420
  31.0 113.5 %copy-start.4 = (f32[2,228,768]{2,1,0:T(8,128)}, f32[2,228,768]{2,1,0:T(8,128)S(1)}, u32[]{:S(2)}) copy-start(f32[2,228,768]{2,1,0:T(8,128)S(1)} %get-tuple-element.231) | copy-start | bytes 4202500
  31.0 94.9 %copy-start.109 = (f32[2,228]{1,0:T(2,128)}, f32[2,228]{1,0:T(2,128)S(1)}, u32[]{:S(2)}) copy-start(f32[2,228]{1,0:T(2,128)S(1)} %broadcast_multiply_fusion.8) | copy-start | bytes 5476
  31.3 94.5 %copy-start.123 = (f32[2,228]{1,0:T(2,128)}, f32[2,228]{1,0:T(2,128)S(1)}, u32[]{:S(2)}) copy-start(f32[2,228]{1,0:T(2,128)S(1)} %fusion.266) | copy-start | bytes 5476
  40.2 107.1 %copy-start.93 = (f32[768]{0:T(1024)}, f32[768]{0:T(1024)S(1)}, u32[]{:S(2)}) copy-start(f32[768]{0:T(1024)S(1)} %get-tuple-element.147) | copy-start | bytes 9220
  40.2 140.4 %copy-start.63 = (f32[768]{0:T(1024)}, f32[768]{0:T(1024)S(1)}, u32[]{:S(2)}) copy-start(f32[768]{0:T(1024)S(1)} %get-tuple-element.146) | copy-start | bytes 9220
  52.9 94.4 %copy-start.106 = (f32[2,228]{1,0:T(2,128)}, f32[2,228]{1,0:T(2,128)S(1)}, u32[]{:S(2)}) copy-start(f32[2,228]{1,0:T(2,128)S(1)} %broadcast_multiply_fusion.11) | copy-start | bytes 5476
  54.3 93.1 %copy-start.113 = (f32[2,228]{1,0:T(2,128)}, f32[2,228]{1,0:T(2,128)S(1)}, u32[]{:S(2)}) copy-start(f32[2,228]{1,0:T(2,128)S(1)} %fusion.263) | copy-start | bytes 5476
  54.9 84.9 %copy-start.104 = (pred[2,228]{1,0:T(4,128)(4,1)}, pred[2,228]{1,0:T(4,128)(4,1)S(1)}, u32[]{:S(2)}) copy-start(pred[2,228]{1,0:T(4,128)(4,1)S(1)} %get-tuple-element.251) | copy-start | bytes 1372
  54.9 104.6 %copy-start.102 = (pred[2,228]{1,0:T(4,128)(4,1)}, pred[2,228]{1,0:T(4,128)(4,1)S(1)}, u32[]{:S(2)}) copy-start(pred[2,228]{1,0:T(4,128)(4,1)S(1)} %get-tuple-element.252) | copy-start | bytes 1372
  186.8 478.7 %copy-start.7 = (f32[2,228,768]{2,1,0:T(8,128)}, f32[2,228,768]{2,1,0:T(8,128)S(1)}, u32[]{:S(2)}) copy-start(f32[2,228,768]{2,1,0:T(8,128)S(1)} %get-tuple-element.212) | copy-start | bytes 4202500
  187.4 72.0 %copy-start.111 = (bf16[2,768]{1,0:T(2,128)(2,1)}, bf16[2,768]{1,0:T(2,128)(2,1)S(1)}, u32[]{:S(2)}) copy-start(bf16[2,768]{1,0:T(2,128)(2,1)S(1)} %multiply_reduce_fusion.22) | copy-start | bytes 9220
  189.8 69.6 %copy-start.129 = (f32[2]{0:T(128)}, f32[2]{0:T(128)S(1)}, u32[]{:S(2)}) copy-start(f32[2]{0:T(128)S(1)} %add_rsqrt_fusion.9) | copy-start | bytes 28
  497.8 90.9 %copy-start.128 = (s32[64]{0:T(128)S(1)}, s32[64]{0:T(128)}, u32[]{:S(2)}) copy-start(s32[64]{0:T(128)} %get-tuple-element.196) | copy-start | bytes 772
  497.9 5.3 collective-permute-start
  502.5 3.6 collective-permute-start.5
  503.2 4.6 collective-permute-start.1
  506.1 4.6 collective-permute-start.6
  507.8 3.0 collective-permute-start.2
  510.8 5.8 collective-permute-start.7
  510.9 4.0 collective-permute-start.3
  514.9 73.8 %collective-permute-start.4 = (bf16[32,1024]{1,0:T(8,128)(2,1)S(1)}, bf16[32,1024]{1,0:T(8,128)(2,1)S(1)}, u32[]{:S(2)}, u32[]{:S(2)}) collective-permute-start(bf16[32,1024]{1,0:T(8,128)(2,1)S(1)} %concatenate.44), channel_id=1, source_target_pairs={{0,16},{1,17},{2,18},{3,19},{4,20},{5,21},{6,22},{7,23},{8,24},{9,... | collective-permute-start | bytes 196616 | tf_op jit(solution)/shard_map/ppermute | solution.py:256
  516.6 71.5 %collective-permute-start.8 = (bf16[16,1024]{1,0:T(8,128)(2,1)S(1)}, bf16[16,1024]{1,0:T(8,128)(2,1)S(1)}, u32[]{:S(2)}, u32[]{:S(2)}) collective-permute-start(bf16[16,1024]{1,0:T(8,128)(2,1)S(1)} %pad_maximum_fusion.3), channel_id=1, source_target_pairs={{0,24},{1,25},{2,26},{3,27},{4,28},{5,29},{6,30},{7,31},{8,0},{9,1... | collective-permute-start | bytes 98312 | tf_op jit(solution)/shard_map/ppermute | solution.py:256
  588.2 71.6 %collective-permute-start.9 = (bf16[32,1024]{1,0:T(8,128)(2,1)S(1)}, bf16[32,1024]{1,0:T(8,128)(2,1)S(1)}, u32[]{:S(2)}, u32[]{:S(2)}) collective-permute-start(bf16[32,1024]{1,0:T(8,128)(2,1)S(1)} %concatenate.49), channel_id=1, source_target_pairs={{0,16},{1,17},{2,18},{3,19},{4,20},{5,21},{6,22},{7,23},{8,24},{9,... | collective-permute-start | bytes 196616 | tf_op jit(solution)/shard_map/ppermute | solution.py:256
  593.5 66.3 %copy-start.127 = (s32[64]{0:T(128)S(1)}, s32[64]{0:T(128)}, u32[]{:S(2)}) copy-start(s32[64]{0:T(128)} %get-tuple-element.195) | copy-start | bytes 772
  740.0 80.0 %reduce-scatter.14.cloned.1.call-start = ((), (), s32[]{:S(2)}) async-start(), calls=%async_computation.18 | async-start | bytes 2654208 | tf_op jit(solution)/shard_map/reduce_scatter | solution.py:305
  744.6 125.4 %reduce-scatter.20.cloned.1.call-start = ((), (), s32[]{:S(2)}) async-start(), calls=%async_computation.21 | async-start | bytes 3538944 | tf_op jit(solution)/shard_map/reduce_scatter | solution.py:308
  748.9 190.0 %reduce-scatter.12.cloned.1.call-start = ((), (), s32[]{:S(2)}) async-start(), calls=%async_computation.17 | async-start | bytes 7962624 | tf_op jit(solution)/shard_map/reduce_scatter | solution.py:304
  759.0 260.1 %reduce-scatter.18.cloned.1.call-start = ((), (), s32[]{:S(2)}) async-start(), calls=%async_computation.20 | async-start | bytes 10616832 | tf_op jit(solution)/shard_map/reduce_scatter | solution.py:307
  775.8 323.6 %reduce-scatter.16.cloned.1.call-start = ((), (), s32[]{:S(2)}) async-start(), calls=%async_computation.19 | async-start | bytes 10616832 | tf_op jit(solution)/shard_map/reduce_scatter | solution.py:306
  787.4 349.7 %reduce-scatter.24.cloned.1.call-start = ((), (), s32[]{:S(2)}) async-start(), calls=%async_computation.23 | async-start | bytes 442368
  788.5 502.9 %all-reduce.3.cloned.1.call-start = ((), (), s32[]{:S(2)}) async-start(), calls=%async_computation.24 | async-start | bytes 8060928 | tf_op jit(solution)/shard_map/psum | solution.py:312
  1099.4 220.5 %copy-start.126 = (f32[3,96]{1,0:T(4,128)S(1)}, f32[3,96]{1,0:T(4,128)}, u32[]{:S(2)}) copy-start(f32[3,96]{1,0:T(4,128)} %param.49) | copy-start | bytes 3460
  1099.5 220.5 %copy-start.133 = (f32[3,96]{1,0:T(4,128)S(1)}, f32[3,96]{1,0:T(4,128)}, u32[]{:S(2)}) copy-start(f32[3,96]{1,0:T(4,128)} %param.56) | copy-start | bytes 3460
  1099.5 220.5 %copy-start.134 = (f32[3,96]{1,0:T(4,128)S(1)}, f32[3,96]{1,0:T(4,128)}, u32[]{:S(2)}) copy-start(f32[3,96]{1,0:T(4,128)} %param.63) | copy-start | bytes 3460
  1099.5 221.2 %copy-start.61 = (f32[96,1024]{1,0:T(8,128)S(1)}, f32[96,1024]{1,0:T(8,128)}, u32[]{:S(2)}) copy-start(f32[96,1024]{1,0:T(8,128)} %param.48) | copy-start | bytes 1179652
  1099.5 221.1 %copy-start.82 = (f32[96,1024]{1,0:T(8,128)S(1)}, f32[96,1024]{1,0:T(8,128)}, u32[]{:S(2)}) copy-start(f32[96,1024]{1,0:T(8,128)} %param.55) | copy-start | bytes 1179652
  (132 other events, 599.5 us)
Sparse Core Ops, SparseCore 0:
  10.5 38.2 all-gather.15
  51.2 24.0 all-gather.17
  77.8 38.9 all-gather.19
  119.1 38.9 all-gather.21
  160.4 25.6 all-gather.23
  187.9 60.4 all-gather.25
  250.3 32.8 all-gather.27
  285.1 74.3 all-gather.29
  361.3 74.3 all-gather.31
  437.5 30.1 all-gather.33
  740.1 34.0 reduce-scatter.21
  777.4 42.4 reduce-scatter.13
  823.7 46.2 reduce-scatter.19
  873.4 65.5 reduce-scatter.11
  942.7 76.4 reduce-scatter.17
  1022.9 76.4 reduce-scatter.15
  1103.2 33.8 reduce-scatter.23
  1140.0 151.4 all-reduce.2
